TPU v7x, 32 devices: a whole 2x2x4 slice. The times are simulated.
32 devices in a mesh: ctx: 8 (over y, x, core), wt: 4 (over z).
Axes of the slice: x: 2, y: 2, z: 4, core: 2. Of those that a mesh axis runs over, the one named last changes fastest.
Arguments:
- words: bfloat16 [6144, 512], P(('ctx', 'wt')), may hold values from -6 to 6
- teacher: bfloat16 [6144, 512], P(('ctx', 'wt')), may hold values from -6 to 6
- valid: int32 [6144], P(('ctx', 'wt')), may hold values from 0 to 1, as said below
- lengths: int32 [4], replicated, may hold values from 384 to 3072, as said below
- deal: int32 [32], replicated, may hold values from 0 to 31, as said below
- gain_attn: bfloat16 [512], P('wt'), may hold values from 0.25 to 1.75
- shift_attn: bfloat16 [512], P('wt'), may hold values from -3 to 3
- w_qkv: bfloat16 [512, 1536], P('wt'), may hold values from -0.25 to 0.25
- w_out: bfloat16 [512, 512], P('wt'), may hold values from -2 to 2
- gain_mlp: bfloat16 [512], P('wt'), may hold values from 0.25 to 1.75
- shift_mlp: bfloat16 [512], P('wt'), may hold values from -3 to 3
- w_up: bfloat16 [512, 2048], P('wt'), may hold values from -0.25 to 0.25
- w_down: bfloat16 [2048, 512], P('wt'), may hold values from -0.125 to 0.125
Outputs:
- layer_out: bfloat16 [6144, 512], P(('ctx', 'wt'))
- loss: float32 [], replicated
- grad_words: float32 [6144, 512], P(('ctx', 'wt'))
- grad_gain_attn: float32 [512], P('wt')
- grad_shift_attn: float32 [512], P('wt')
- grad_w_qkv: float32 [512, 1536], P('wt')
- grad_w_out: float32 [512, 512], P('wt')
- grad_gain_mlp: float32 [512], P('wt')
- grad_shift_mlp: float32 [512], P('wt')
- grad_w_up: float32 [512, 2048], P('wt')
- grad_w_down: float32 [2048, 512], P('wt')
Inputs may be any that keep to these rules, and one draw needn't show every extreme that they name: lengths are multiples of 192 that sum to 6144; one sequence has exactly 3072 words. `deal`: each initial block appears once; initial blocks that differ by a multiple of the number of ctx indices lie on the same ctx index. The first word of every dealt block is valid.
All inputs are finite; a program needn't handle non-finite values.
Results may differ from a plain program's by a relative error of at most 0.02.
Values may be sent and summed in bfloat16 or wider, within the bound.
No kernel may reach another device: no remote copies, remote signals or barrier semaphores. Data moves between devices by JAX's collectives and lax.ppermute only.
A program may use at most 128 MiB of HBM per device.

v0:
```python
import jax
import jax.numpy as jnp
from jax import lax
from jax.sharding import PartitionSpec as P

H = 8
HEAD = 64
EPS = 1e-05
LOSS_SCALE = 262144.0


def norm_forward(values, gain_vec, shift_vec):
    center = values - jnp.mean(values, axis=-1, keepdims=True)
    inverse = lax.rsqrt(jnp.mean(center * center, axis=-1, keepdims=True) + EPS)
    unit_rows = center * inverse
    return (unit_rows * gain_vec + shift_vec, unit_rows, inverse)


def norm_backward(upstream, unit_rows, inverse, gain_vec):
    scaled = upstream * gain_vec
    inner_term = jnp.mean(scaled * unit_rows, axis=-1, keepdims=True)
    result = inverse * (scaled - jnp.mean(scaled, axis=-1, keepdims=True) - unit_rows * inner_term)
    return (result, jnp.sum(upstream * unit_rows, axis=0), jnp.sum(upstream, axis=0))


def per_device(
    words,
    teacher,
    valid,
    lengths,
    deal,
    gain_attn,
    shift_attn,
    w_qkv,
    w_out,
    gain_mlp,
    shift_mlp,
    w_up,
    w_down,
):
    ctx_count = lax.axis_size("ctx")
    wt_count = lax.axis_size("wt")
    blk_rows = words.shape[0]
    model_width = words.shape[1]
    head_count = H // wt_count
    col_span = 3 * head_count * HEAD
    group_rows = blk_rows * wt_count
    score_scale = HEAD ** (-0.5)
    qkv_full, out_full, gain_first_raw, shift_first_raw = (
        lax.all_gather(w_qkv, "wt", axis=0, tiled=True),
        lax.all_gather(w_out, "wt", axis=0, tiled=True),
        lax.all_gather(gain_attn, "wt", axis=0, tiled=True),
        lax.all_gather(shift_attn, "wt", axis=0, tiled=True),
    )
    qkv_grouped = qkv_full.reshape(model_width, wt_count, col_span)
    out_grouped = out_full.reshape(wt_count, head_count * HEAD, model_width)
    gain_first = gain_first_raw.astype(jnp.float32)
    shift_first = shift_first_raw.astype(jnp.float32)
    inputs = words.astype(jnp.float32)
    normed_one, unit_first, inverse_first = norm_forward(inputs, gain_first, shift_first)
    packed_first = normed_one.astype(jnp.bfloat16)
    projected = jnp.einsum(
        "rd,dwc->wrc", packed_first, qkv_grouped, preferred_element_type=jnp.float32
    ).astype(jnp.bfloat16)
    head_rows = lax.all_to_all(
        projected.reshape(wt_count, blk_rows * col_span),
        "wt",
        split_axis=0,
        concat_axis=0,
        tiled=True,
    )
    head_rows = head_rows.reshape(group_rows, head_count, 3, HEAD)
    queries = head_rows[:, :, 0]
    own_kv = head_rows[:, :, 1:]
    key_values = own_kv.reshape(group_rows, head_count * 2 * HEAD)
    gathered = lax.all_gather(key_values, "ctx", axis=0, tiled=True).reshape(
        ctx_count, group_rows, head_count, 2, HEAD
    )
    offsets = jnp.arange(blk_rows, dtype=jnp.int32)
    bounds = jnp.cumsum(lengths)
    key_place = (deal[:, None] * blk_rows + offsets[None, :]).reshape(ctx_count, group_rows)
    key_seq = jnp.sum((key_place[:, :, None] >= bounds[None, None, :]).astype(jnp.int32), axis=-1)
    ctx_here = lax.axis_index("ctx")
    query_place = lax.dynamic_index_in_dim(key_place, ctx_here, 0, keepdims=False)
    query_seq = lax.dynamic_index_in_dim(key_seq, ctx_here, 0, keepdims=False)
    live_pieces = jnp.ones((ctx_count,), dtype=bool)
    scan_items = (gathered, key_place, key_seq, live_pieces)

    def scores_of(kv_piece, piece_place, piece_seq):
        raw_scores = (
            jnp.einsum(
                "qhd,khd->hqk", queries, kv_piece[:, :, 0], preferred_element_type=jnp.float32
            )
            * score_scale
        )
        visible = (piece_seq[None, :] == query_seq[:, None]) & (
            piece_place[None, :] <= query_place[:, None]
        )
        return (raw_scores, visible[None])

    def forward_step(carry, item):
        kv_piece, piece_place, piece_seq, live_piece = item
        running_max, running_sum, running_acc = carry
        raw_scores, visible = scores_of(kv_piece, piece_place, piece_seq)
        piece_max = jnp.max(jnp.where(visible, raw_scores, -1e30), axis=-1)
        new_max = jnp.maximum(running_max, piece_max)
        weights = jnp.where(visible, jnp.exp(raw_scores - new_max[..., None]), 0.0)
        factor = jnp.exp(running_max - new_max)
        new_sum = running_sum * factor + jnp.sum(weights, axis=-1)
        new_acc = running_acc * factor.T[:, :, None] + jnp.einsum(
            "hqk,khd->qhd",
            weights.astype(jnp.bfloat16),
            kv_piece[:, :, 1],
            preferred_element_type=jnp.float32,
        )
        return ((new_max, new_sum, new_acc), None)

    start_max = jnp.full((head_count, group_rows), -1e30, jnp.float32)
    start_sum = jnp.zeros((head_count, group_rows), jnp.float32)
    start_acc = jnp.zeros((group_rows, head_count, HEAD), jnp.float32)
    (row_max, row_sum, row_acc), _ = lax.scan(
        forward_step, (start_max, start_sum, start_acc), scan_items
    )
    log_total = row_max + jnp.log(row_sum)
    attended_full = row_acc / row_sum.T[:, :, None]
    attended_heads = attended_full.astype(jnp.bfloat16)
    attended_rows = lax.all_to_all(
        attended_heads.reshape(wt_count, blk_rows * head_count * HEAD),
        "wt",
        split_axis=0,
        concat_axis=0,
        tiled=True,
    ).reshape(wt_count, blk_rows, head_count * HEAD)
    residual_one = inputs + jnp.einsum(
        "wrc,wcd->rd", attended_rows, out_grouped, preferred_element_type=jnp.float32
    )
    up_full, down_full, gain_second_raw, shift_second_raw = (
        lax.all_gather(w_up, "wt", axis=0, tiled=True),
        lax.all_gather(w_down, "wt", axis=0, tiled=True),
        lax.all_gather(gain_mlp, "wt", axis=0, tiled=True),
        lax.all_gather(shift_mlp, "wt", axis=0, tiled=True),
    )
    gain_second = gain_second_raw.astype(jnp.float32)
    shift_second = shift_second_raw.astype(jnp.float32)
    normed_two, unit_second, inverse_second = norm_forward(residual_one, gain_second, shift_second)
    packed_second = normed_two.astype(jnp.bfloat16)
    before_act = jnp.dot(packed_second, up_full, preferred_element_type=jnp.float32)
    activated = jax.nn.gelu(before_act, approximate=False).astype(jnp.bfloat16)
    residual_two = residual_one + jnp.dot(activated, down_full, preferred_element_type=jnp.float32)
    distance = residual_two - teacher.astype(jnp.float32)
    valid_float = valid.astype(jnp.float32)
    count_all, square_all = lax.psum(
        (jnp.sum(valid_float), jnp.sum(valid_float * jnp.sum(distance * distance, axis=-1))),
        ("ctx", "wt"),
    )
    loss_value = square_all / (count_all * model_width)
    grad_two = 2.0 * LOSS_SCALE / (count_all * model_width) * valid_float[:, None] * distance
    grad_branch = grad_two.astype(jnp.bfloat16)
    grad_down = jnp.einsum("rf,rd->fd", activated, grad_branch, preferred_element_type=jnp.float32)
    grad_act = jnp.einsum("rd,fd->rf", grad_branch, down_full, preferred_element_type=jnp.float32)
    _, gelu_back = jax.vjp(lambda hidden_in: jax.nn.gelu(hidden_in, approximate=False), before_act)
    grad_pre = gelu_back(grad_act)[0].astype(jnp.bfloat16)
    grad_up = jnp.einsum("rd,rf->df", packed_second, grad_pre, preferred_element_type=jnp.float32)
    grad_normed_two = jnp.einsum("rf,df->rd", grad_pre, up_full, preferred_element_type=jnp.float32)
    back_two, grad_gain_second, grad_shift_second = norm_backward(
        grad_normed_two, unit_second, inverse_second, gain_second
    )
    grad_one = grad_two + back_two
    grad_attn_out = grad_one.astype(jnp.bfloat16)
    grad_out = jnp.einsum(
        "wrc,rd->wcd", attended_rows, grad_attn_out, preferred_element_type=jnp.float32
    ).reshape(model_width, model_width)
    grad_att_rows = jnp.einsum(
        "rd,wcd->wrc", grad_attn_out, out_grouped, preferred_element_type=jnp.float32
    ).astype(jnp.bfloat16)
    grad_att_heads = lax.all_to_all(
        grad_att_rows.reshape(wt_count, blk_rows * head_count * HEAD),
        "wt",
        split_axis=0,
        concat_axis=0,
        tiled=True,
    ).reshape(group_rows, head_count, HEAD)
    row_delta = jnp.sum(grad_att_heads.astype(jnp.float32) * attended_full, axis=-1).T

    def score_grads(kv_piece, piece_place, piece_seq):
        raw_scores, visible = scores_of(kv_piece, piece_place, piece_seq)
        probs = jnp.where(visible, jnp.exp(raw_scores - log_total[..., None]), 0.0)
        grad_probs = jnp.einsum(
            "qhd,khd->hqk", grad_att_heads, kv_piece[:, :, 1], preferred_element_type=jnp.float32
        )
        return (probs, (probs * (grad_probs - row_delta[..., None])).astype(jnp.bfloat16))

    def grad_step(carry, item):
        kv_piece, piece_place, piece_seq, live_piece = item
        probs, grad_scores = score_grads(kv_piece, piece_place, piece_seq)
        grad_keys = (
            jnp.einsum("hqk,qhd->khd", grad_scores, queries, preferred_element_type=jnp.float32)
            * score_scale
        )
        grad_values = jnp.einsum(
            "hqk,qhd->khd",
            probs.astype(jnp.bfloat16),
            grad_att_heads,
            preferred_element_type=jnp.float32,
        )
        grad_next = carry + jnp.einsum(
            "hqk,khd->qhd", grad_scores, kv_piece[:, :, 0], preferred_element_type=jnp.float32
        )
        return (grad_next, jnp.stack([grad_keys, grad_values], axis=2))

    grad_query_sum, grad_pieces = lax.scan(
        grad_step, jnp.zeros((group_rows, head_count, HEAD), jnp.float32), scan_items
    )
    grad_kv = lax.psum_scatter(
        grad_pieces.reshape(ctx_count * group_rows, head_count * 2 * HEAD).astype(jnp.bfloat16),
        "ctx",
        scatter_dimension=0,
        tiled=True,
    ).astype(jnp.float32)
    grad_kv = grad_kv.astype(jnp.bfloat16).reshape(group_rows, head_count, 2, HEAD)
    grad_queries = (grad_query_sum * score_scale).astype(jnp.bfloat16)
    grad_heads = jnp.concatenate([grad_queries[:, :, None], grad_kv], axis=2)
    grad_rows = lax.all_to_all(
        grad_heads.reshape(wt_count, blk_rows * col_span),
        "wt",
        split_axis=0,
        concat_axis=0,
        tiled=True,
    ).reshape(wt_count, blk_rows, col_span)
    grad_qkv = jnp.einsum(
        "rd,wrc->dwc", packed_first, grad_rows, preferred_element_type=jnp.float32
    ).reshape(model_width, 3 * model_width)
    grad_normed_one = jnp.einsum(
        "wrc,dwc->rd", grad_rows, qkv_grouped, preferred_element_type=jnp.float32
    )
    back_one, grad_gain_first, grad_shift_first = norm_backward(
        grad_normed_one, unit_first, inverse_first, gain_first
    )
    grad_words = grad_one + back_one
    shard_ga, shard_sa, shard_qkv, shard_out, shard_gm, shard_sm, shard_up, shard_down = (
        lax.psum_scatter(
            grad_gain_first.astype(jnp.bfloat16), "wt", scatter_dimension=0, tiled=True
        ).astype(jnp.float32),
        lax.psum_scatter(
            grad_shift_first.astype(jnp.bfloat16), "wt", scatter_dimension=0, tiled=True
        ).astype(jnp.float32),
        lax.psum_scatter(
            grad_qkv.astype(jnp.bfloat16), "wt", scatter_dimension=0, tiled=True
        ).astype(jnp.float32),
        lax.psum_scatter(
            grad_out.astype(jnp.bfloat16), "wt", scatter_dimension=0, tiled=True
        ).astype(jnp.float32),
        lax.psum_scatter(
            grad_gain_second.astype(jnp.bfloat16), "wt", scatter_dimension=0, tiled=True
        ).astype(jnp.float32),
        lax.psum_scatter(
            grad_shift_second.astype(jnp.bfloat16), "wt", scatter_dimension=0, tiled=True
        ).astype(jnp.float32),
        lax.psum_scatter(
            grad_up.astype(jnp.bfloat16), "wt", scatter_dimension=0, tiled=True
        ).astype(jnp.float32),
        lax.psum_scatter(
            grad_down.astype(jnp.bfloat16), "wt", scatter_dimension=0, tiled=True
        ).astype(jnp.float32),
    )
    summed = (
        lax.psum(shard_ga.astype(jnp.bfloat16), "ctx").astype(jnp.float32),
        lax.psum(shard_sa.astype(jnp.bfloat16), "ctx").astype(jnp.float32),
        lax.psum(shard_qkv.astype(jnp.bfloat16), "ctx").astype(jnp.float32),
        lax.psum(shard_out.astype(jnp.bfloat16), "ctx").astype(jnp.float32),
        lax.psum(shard_gm.astype(jnp.bfloat16), "ctx").astype(jnp.float32),
        lax.psum(shard_sm.astype(jnp.bfloat16), "ctx").astype(jnp.float32),
        lax.psum(shard_up.astype(jnp.bfloat16), "ctx").astype(jnp.float32),
        lax.psum(shard_down.astype(jnp.bfloat16), "ctx").astype(jnp.float32),
    )
    return (
        residual_two.astype(jnp.bfloat16),
        loss_value,
        grad_words,
        summed[0],
        summed[1],
        summed[2],
        summed[3],
        summed[4],
        summed[5],
        summed[6],
        summed[7],
    )


def solution(mesh):
    placed = (
        P(("ctx", "wt"), None),
        P(("ctx", "wt"), None),
        P(("ctx", "wt")),
        P(),
        P(),
        P("wt"),
        P("wt"),
        P("wt", None),
        P("wt", None),
        P("wt"),
        P("wt"),
        P("wt", None),
        P("wt", None),
    )
    return jax.shard_map(
        per_device,
        mesh=mesh,
        in_specs=placed,
        out_specs=(
            P(("ctx", "wt"), None),
            P(),
            P(("ctx", "wt"), None),
            P("wt"),
            P("wt"),
            P("wt", None),
            P("wt", None),
            P("wt"),
            P("wt"),
            P("wt", None),
            P("wt", None),
        ),
        check_vma=False,
    )
```

profile of v0, /device:TPU:0, one launch (start us, length us, event | category | flops | bytes accessed | tf_op | source)
XLA Modules:
  0.0 679.7 jit_solution(10840386280325061220)
XLA Ops:
  9.3 12.7 %all-gather = bf16[4,1,128]{2,1,0:T(2,128)(2,1)S(1)} all-gather(bf16[1,1,128]{2,1,0:T(2,128)(2,1)} %bitcast.256), channel_id=1, replica_groups=mesh['ctx'=8,'wt'=4] {'wt'}, dimensions={0}, use_global_device_ids=true | all-gather | bytes 1280 | tf_op jit(solution)/shard_map/all_gather | solution.py:52
  22.0 7.8 %all-gather.1 = bf16[4,1,128]{2,1,0:T(2,128)(2,1)S(1)} all-gather(bf16[1,1,128]{2,1,0:T(2,128)(2,1)} %bitcast.257), channel_id=1, replica_groups=mesh['ctx'=8,'wt'=4] {'wt'}, dimensions={0}, use_global_device_ids=true | all-gather | bytes 1280 | tf_op jit(solution)/shard_map/all_gather | solution.py:53
  32.0 18.6 %all-gather.9.cloned.1.call-done = bf16[512,1536]{0,1:T(8,128)(2,1)} async-done(((bf16[128,1536]{0,1:T(8,128)(2,1)}), bf16[512,1536]{0,1:T(8,128)(2,1)}) %all-gather.9.cloned.1.call-update) | async-done | bytes 1572880 | tf_op jit(solution)/shard_map/all_gather | solution.py:50
  53.6 4.4 reduce.16
  58.6 18.8 %all_to_all.40 = bf16[4,2,36864]{2,1,0:T(2,128)(2,1)S(1)} all-to-all(bf16[4,2,36864]{2,1,0:T(2,128)(2,1)S(1)} %reshape.330), channel_id=1, replica_groups=mesh['ctx'=8,'wt'=4] {'wt'}, dimensions={0} | all-to-all | bytes 1179648 | tf_op jit(solution)/shard_map/all_to_all | solution.py:65
  78.0 3.8 reduce.6
  90.4 26.7 %all-gather.11.cloned.1.call-done = bf16[6144,256]{0,1:T(8,128)(2,1)} async-done(((bf16[768,256]{0,1:T(8,128)(2,1)}), bf16[6144,256]{0,1:T(8,128)(2,1)}) %all-gather.11.cloned.1.call-update) | async-done | bytes 3145744 | tf_op jit(solution)/shard_map/all_gather | solution.py:76
  117.1 2.8 copy.143
  122.3 84.7 %while.28 = (s32[]{:T(128)}, f32[2,768]{1,0:T(2,128)S(1)}, f32[2,768]{1,0:T(2,128)S(1)}, f32[768,2,64]{0,2,1:T(8,128)S(1)}, s32[8,768]{1,0:T(8,128)}, /*index=5*...) while((s32[]{:T(128)}, f32[2,768]{1,0:T(2,128)S(1)}, ...), condition=%wide.region_7.8_spmd.clone, body=%wide.region_4.7_spmd.clone.sunk | while | flops 317039616 | bytes 37675172 | solution.py:121
  124.6 3.2 fusion.119
  127.8 3.8 fusion.123
  135.2 3.2 fusion.119
  138.4 3.8 fusion.123
  145.7 3.2 fusion.119
  148.9 3.8 fusion.123
  156.3 3.2 fusion.119
  159.5 3.8 fusion.123
  166.8 3.2 fusion.119
  170.0 4.1 fusion.123
  177.8 3.2 fusion.119
  181.0 3.8 fusion.123
  188.3 3.2 fusion.119
  191.5 3.9 fusion.123
  198.9 3.2 fusion.119
  202.1 3.8 fusion.123
  213.4 4.5 all-to-all-start.1
  217.9 11.3 %all-gather.2 = bf16[4,1,128]{2,1,0:T(2,128)(2,1)S(1)} all-gather(bf16[1,1,128]{2,1,0:T(2,128)(2,1)S(1)} %bitcast.258), channel_id=1, replica_groups=mesh['ctx'=8,'wt'=4] {'wt'}, dimensions={0}, use_global_device_ids=true | all-gather | bytes 1280 | tf_op jit(solution)/shard_map/all_gather | solution.py:140
  229.2 7.7 %all-gather.3 = bf16[4,1,128]{2,1,0:T(2,128)(2,1)S(1)} all-gather(bf16[1,1,128]{2,1,0:T(2,128)(2,1)S(1)} %bitcast.259), channel_id=1, replica_groups=mesh['ctx'=8,'wt'=4] {'wt'}, dimensions={0}, use_global_device_ids=true | all-gather | bytes 1280 | tf_op jit(solution)/shard_map/all_gather | solution.py:141
  236.9 15.2 %all_gather.31 = bf16[512,512]{1,0:T(8,128)(2,1)S(1)} all-gather(bf16[128,512]{1,0:T(8,128)(2,1)S(1)} %copy-done.20), channel_id=1, replica_groups=mesh['ctx'=8,'wt'=4] {'wt'}, dimensions={0}, use_global_device_ids=true | all-gather | bytes 655360 | tf_op jit(solution)/shard_map/all_gather | solution.py:51
  254.2 6.9 %multiply_convert_fusion = (bf16[192,2048]{1,0:T(8,128)(2,1)}, f32[192,2048]{1,0:T(8,128)}, f32[192,2048]{1,0:T(8,128)}) fusion(bf16[512,2048]{1,0:T(8,128)(2,1)} %all-gather.13.cloned.1.call-done, f32[192,512]{1,0:T(8,128)S(1)} %get-tuple-element.400, f32[512]{0:T(512)S(1)} %bitcast.253, f32[512]{0:T(512)S(1)} %bitcast.249, f32[192]{0:T(256)S(1)} %add_rsqrt_fusion, ...), kind=kOutput, calls=%fused_computation.55 | convolution fusion | flops 428703744 | bytes 6428160 | tf_op jit(solution)/shard_map/dot_general | solution.py:147
  261.1 2.5 multiply_reduce_fusion.3
  264.3 38.9 %all-reduce.4 = (f32[]{:T(128)}, f32[]{:T(128)}) all-reduce(f32[]{:T(128)} %get-tuple-element.324, f32[]{:T(128)} %get-tuple-element.323), channel_id=1, replica_groups=mesh['ctx'=8,'wt'=4] {'ctx','wt'}, use_global_device_ids=true, to_apply=%region_12.13 | all-reduce | flops 2 | bytes 16 | tf_op jit(solution)/shard_map/psum | solution.py:152
  304.0 3.7 add_convert_fusion
  313.3 3.8 all-to-all-start.2
  318.0 5.9 all-to-all-done.2
  328.3 66.9 %while.29 = (s32[]{:T(128)}, f32[768,2,64]{0,2,1:T(8,128)S(1)}, bf16[8,768,2,2,64]{1,4,2,3,0:T(8,128)(2,1)}, bf16[8,768,2,2,64]{1,4,2,3,0:T(8,128)(2,1)}, s32[8,...) while((s32[]{:T(128)}, f32[768,2,64]{0,2,1:T(8,128)S(1)}, ...), condition=%wide.region_19.20_spmd.clone, body=%wide.region_18.19_spmd.clone.sunk | while | flops 769720320 | bytes 28011244 | solution.py:211
  395.1 3.6 copy.129
  398.8 2.6 copy.145
  409.4 38.5 %reduce-scatter.6.cloned.1.call-done = bf16[768,256]{0,1:T(8,128)(2,1)} async-done(((bf16[6144,256]{0,1:T(8,128)(2,1)}), bf16[768,256]{0,1:T(8,128)(2,1)}) %reduce-scatter.6.cloned.1.call-update) | async-done | bytes 393232 | tf_op jit(solution)/shard_map/reduce_scatter | solution.py:214
  452.1 5.6 reduce.19
  458.3 23.0 %all_to_all.41 = bf16[4,2,36864]{2,1,0:T(2,128)(2,1)S(1)} all-to-all(bf16[4,2,36864]{2,1,0:T(2,128)(2,1)S(1)} %reshape.336), channel_id=1, replica_groups=mesh['ctx'=8,'wt'=4] {'wt'}, dimensions={0} | all-to-all | bytes 1179648 | tf_op jit(solution)/shard_map/all_to_all | solution.py:223
  481.9 3.8 reduce.9
  490.3 31.3 %reduce-scatter.12.cloned.1.call-done = bf16[128,2048]{1,0:T(8,128)(2,1)} async-done(((bf16[512,2048]{1,0:T(8,128)(2,1)}), bf16[128,2048]{1,0:T(8,128)(2,1)}) %reduce-scatter.12.cloned.1.call-update) | async-done | bytes 524304 | tf_op jit(solution)/shard_map/reduce_scatter | solution.py:259
  521.7 45.5 %reduce-scatter.14.cloned.1.call-done = bf16[512,512]{1,0:T(8,128)(2,1)} async-done(((bf16[2048,512]{1,0:T(8,128)(2,1)}), bf16[512,512]{1,0:T(8,128)(2,1)}) %reduce-scatter.14.cloned.1.call-update) | async-done | bytes 524304 | tf_op jit(solution)/shard_map/reduce_scatter | solution.py:262
  567.2 37.1 %reduce-scatter.8.cloned.1.call-done = bf16[128,1536]{1,0:T(8,128)(2,1)} async-done(((bf16[512,1536]{1,0:T(8,128)(2,1)}), bf16[128,1536]{1,0:T(8,128)(2,1)}) %reduce-scatter.8.cloned.1.call-update) | async-done | bytes 393232 | tf_op jit(solution)/shard_map/reduce_scatter | solution.py:247
  606.4 9.8 %all-reduce.7 = (bf16[512]{0:T(512)(128)(2,1)S(1)}, bf16[512]{0:T(512)(128)(2,1)S(1)}, bf16[512]{0:T(512)(128)(2,1)S(1)}, bf16[512]{0:T(512)(128)(2,1)S(1)}) all-reduce(bf16[512]{0:T(512)(128)(2,1)S(1)} %get-tuple-element.317, bf16[512]{0:T(512)(128)(2,1)S(1)} %get-tuple-element.322, ...), channel_id=3, replica_groups=mesh['ctx'=8,'wt'=4] {'wt'}, use_global_device_ids=true, to_apply=%region_24.25.clone | all-reduce | flops 2048 | bytes 8192
  616.5 11.9 %all-reduce.5 = (bf16[128]{0:T(256)(128)(2,1)S(1)}, bf16[128]{0:T(256)(128)(2,1)S(1)}, bf16[128]{0:T(256)(128)(2,1)S(1)}, bf16[128]{0:T(256)(128)(2,1)S(1)}) all-reduce(bf16[128]{0:T(256)(128)(2,1)S(1)} %dynamic-slice.1, bf16[128]{0:T(256)(128)(2,1)S(1)} %dynamic-slice.3, ...), channel_id=1, replica_groups=mesh['ctx'=8,'wt'=4] {'ctx'}, use_global_device_ids=true, to_apply=%region_25.26 | all-reduce | flops 512 | bytes 2048 | tf_op jit(solution)/shard_map/psum | solution.py:267
  631.3 35.2 %all-reduce.10.cloned.1.call-done = (bf16[128,1536]{1,0:T(8,128)(2,1)}, bf16[128,512]{1,0:T(8,128)(2,1)}, bf16[128,2048]{1,0:T(8,128)(2,1)}, bf16[512,512]{1,0:T(8,128)(2,1)}) async-done(((bf16[128,1536]{1,0:T(8,128)(2,1)}, bf16[128,512]{1,0:T(8,128)(2,1)}, bf16[128,2048]{1,0:T(8,128)(2,1)}, bf16[512,512]{1,0:T(8,128)(2,1)}), (bf16[128,1536]{1,0:T(8,128)(2,1)}, bf16[128,512]{1,0:T(8,128)(2,1)}, ...) | async-done | bytes 1572880 | tf_op jit(solution)/shard_map/psum | solution.py:269
  (402 shorter events, 160.1 us)
Async XLA Ops:
  7.2 43.5 %copy-start.3 = (bf16[192,512]{1,0:T(8,128)(2,1)S(1)}, bf16[192,512]{1,0:T(8,128)(2,1)}, u32[]{:S(2)}) copy-start(bf16[192,512]{1,0:T(8,128)(2,1)} %param.17) | copy-start | bytes 589828
  7.2 43.4 %all-gather.9.cloned.1.call-start = ((), (), s32[]{:S(2)}) async-start(), calls=%async_computation.9 | async-start | bytes 1966080 | tf_op jit(solution)/shard_map/all_gather | solution.py:50
  9.2 107.9 %all-gather.11.cloned.1.call-start = ((), (), s32[]{:S(2)}) async-start(), calls=%async_computation.10 | async-start | bytes 3538944 | tf_op jit(solution)/shard_map/all_gather | solution.py:76
  22.0 28.6 %copy-start.22 = (f32[4,1,128]{2,1,0:T(1,128)}, f32[4,1,128]{2,1,0:T(1,128)S(1)}, u32[]{:S(2)}) copy-start(f32[4,1,128]{2,1,0:T(1,128)S(1)} %convert_element_type.187) | copy-start | bytes 6148
  29.8 20.8 %copy-start.26 = (f32[4,1,128]{2,1,0:T(1,128)}, f32[4,1,128]{2,1,0:T(1,128)S(1)}, u32[]{:S(2)}) copy-start(f32[4,1,128]{2,1,0:T(1,128)S(1)} %convert_element_type.188) | copy-start | bytes 6148
  30.8 19.8 %copy-start.24 = (f32[192]{0:T(256)}, f32[192]{0:T(256)S(1)}, u32[]{:S(2)}) copy-start(f32[192]{0:T(256)S(1)} %broadcast_multiply_fusion.5) | copy-start | bytes 2308
  32.0 18.6 %copy-start.32 = (f32[192]{0:T(256)}, f32[192]{0:T(256)S(1)}, u32[]{:S(2)}) copy-start(f32[192]{0:T(256)S(1)} %add_rsqrt_fusion.1) | copy-start | bytes 2308
  83.7 3.1 copy-start.46
  83.7 3.5 copy-start.47
  85.4 168.8 %all-gather.13.cloned.1.call-start = ((), (), s32[]{:S(2)}) async-start(), calls=%async_computation.11 | async-start | bytes 2621440 | tf_op jit(solution)/shard_map/all_gather | solution.py:138
  86.1 175.0 %all-gather.15.cloned.1.call-start = ((), (), s32[]{:S(2)}) async-start(), calls=%async_computation.12 | async-start | bytes 2621440 | tf_op jit(solution)/shard_map/all_gather | solution.py:139
  127.8 3.8 copy-start
  138.4 3.8 copy-start
  148.9 3.8 copy-start
  159.5 3.8 copy-start
  170.0 4.3 copy-start
  181.0 3.8 copy-start
  191.5 3.9 copy-start
  202.1 3.8 copy-start
  207.1 3.3 copy-start.17
  210.4 7.5 %copy-start.43 = (bf16[128]{0:T(256)(128)(2,1)S(1)}, bf16[128]{0:T(256)(128)(2,1)}, u32[]{:S(2)}) copy-start(bf16[128]{0:T(256)(128)(2,1)} %param.26) | copy-start | bytes 772
  210.4 18.9 %copy-start.44 = (bf16[128]{0:T(256)(128)(2,1)S(1)}, bf16[128]{0:T(256)(128)(2,1)}, u32[]{:S(2)}) copy-start(bf16[128]{0:T(256)(128)(2,1)} %param.27) | copy-start | bytes 772
  210.4 26.5 %copy-start.20 = (bf16[128,512]{1,0:T(8,128)(2,1)S(1)}, bf16[128,512]{1,0:T(8,128)(2,1)}, u32[]{:S(2)}) copy-start(bf16[128,512]{1,0:T(8,128)(2,1)} %param.25) | copy-start | bytes 393220
  213.4 38.7 %all-to-all-start.1 = ((bf16[4,2,12288]{2,1,0:T(2,128)(2,1)}), bf16[4,2,12288]{2,1,0:T(2,128)(2,1)S(1)}, u32[]{:S(2)}, u32[]{:S(2)}) async-start(bf16[4,2,12288]{2,1,0:T(2,128)(2,1)} %reshape.332), calls=%async_computation.1 | async-start | bytes 393216 | tf_op jit(solution)/shard_map/all_to_all | solution.py:127
  229.2 80.0 %copy-start.28 = (f32[4,1,128]{2,1,0:T(1,128)}, f32[4,1,128]{2,1,0:T(1,128)S(1)}, u32[]{:S(2)}) copy-start(f32[4,1,128]{2,1,0:T(1,128)S(1)} %convert_element_type.189) | copy-start | bytes 6148
  236.9 17.3 %copy-start.36 = (f32[4,1,128]{2,1,0:T(1,128)}, f32[4,1,128]{2,1,0:T(1,128)S(1)}, u32[]{:S(2)}) copy-start(f32[4,1,128]{2,1,0:T(1,128)S(1)} %convert_element_type.190) | copy-start | bytes 6148
  253.5 7.6 %copy-start.8 = (bf16[4,24576]{1,0:T(4,128)(2,1)}, bf16[4,24576]{1,0:T(4,128)(2,1)S(1)}, u32[]{:S(2)}) copy-start(bf16[4,24576]{1,0:T(4,128)(2,1)S(1)} %reduce.7) | copy-start | bytes 589828
  253.9 55.3 %copy-start.1 = (f32[192,512]{1,0:T(8,128)}, f32[192,512]{1,0:T(8,128)S(1)}, u32[]{:S(2)}) copy-start(f32[192,512]{1,0:T(8,128)S(1)} %get-tuple-element.400) | copy-start | bytes 1179652
  253.9 55.3 %copy-start.30 = (f32[192]{0:T(256)}, f32[192]{0:T(256)S(1)}, u32[]{:S(2)}) copy-start(f32[192]{0:T(256)S(1)} %broadcast_multiply_fusion.4) | copy-start | bytes 2308
  254.1 55.1 %copy-start.34 = (f32[192]{0:T(256)}, f32[192]{0:T(256)S(1)}, u32[]{:S(2)}) copy-start(f32[192]{0:T(256)S(1)} %add_rsqrt_fusion) | copy-start | bytes 2308
  254.2 6.9 %copy-start.7 = (bf16[192,512]{1,0:T(8,128)(2,1)S(1)}, bf16[192,512]{1,0:T(8,128)(2,1)}, u32[]{:S(2)}) copy-start(bf16[192,512]{1,0:T(8,128)(2,1)} %param.18) | copy-start | bytes 589828
  261.1 2.6 copy-start.40
  304.0 3.7 copy-start.10
  304.0 3.7 copy-start.45
  310.1 13.9 %copy-start.4 = (f32[192,512]{1,0:T(8,128)}, f32[192,512]{1,0:T(8,128)S(1)}, u32[]{:S(2)}) copy-start(f32[192,512]{1,0:T(8,128)S(1)} %get-tuple-element.395) | copy-start | bytes 1179652
  310.1 7.2 %copy-start.18 = (f32[2,768]{1,0:T(2,128)S(1)}, f32[2,768]{1,0:T(2,128)}, u32[]{:S(2)}) copy-start(f32[2,768]{1,0:T(2,128)} %copy-done.17) | copy-start | bytes 18436
  313.3 10.5 %all-to-all-start.2 = ((bf16[4,2,12288]{2,1,0:T(2,128)(2,1)}), bf16[4,2,12288]{2,1,0:T(2,128)(2,1)S(1)}, u32[]{:S(2)}, u32[]{:S(2)}) async-start(bf16[4,2,12288]{2,1,0:T(2,128)(2,1)} %reshape.334), calls=%async_computation.2 | async-start | bytes 393216 | tf_op jit(solution)/shard_map/all_to_all | solution.py:176
  317.1 130.7 %reduce-scatter.6.cloned.1.call-start = ((), (), s32[]{:S(2)}) async-start(), calls=%async_computation.13 | async-start | bytes 3538944 | tf_op jit(solution)/shard_map/reduce_scatter | solution.py:214
  401.4 2.2 copy-start.2
  401.4 2.2 copy-start.13
  401.4 2.2 copy-start.29
  401.4 2.2 copy-start.31
  401.5 88.9 %reduce-scatter.10.cloned.1.call-start = ((), (), s32[]{:S(2)}) async-start(), calls=%async_computation.15 | async-start | bytes 655360 | tf_op jit(solution)/shard_map/reduce_scatter | solution.py:250
  403.6 118.1 %reduce-scatter.12.cloned.1.call-start = ((), (), s32[]{:S(2)}) async-start(), calls=%async_computation.16 | async-start | bytes 2621440 | tf_op jit(solution)/shard_map/reduce_scatter | solution.py:259
  405.9 161.3 %reduce-scatter.14.cloned.1.call-start = ((), (), s32[]{:S(2)}) async-start(), calls=%async_computation.17 | async-start | bytes 2621440 | tf_op jit(solution)/shard_map/reduce_scatter | solution.py:262
  409.3 195.0 %reduce-scatter.8.cloned.1.call-start = ((), (), s32[]{:S(2)}) async-start(), calls=%async_computation.14 | async-start | bytes 1966080 | tf_op jit(solution)/shard_map/reduce_scatter | solution.py:247
  488.4 178.2 %all-reduce.10.cloned.1.call-start = ((), (), s32[]{:S(2)}) async-start(), calls=%async_computation.18 | async-start | bytes 3145728 | tf_op jit(solution)/shard_map/psum | solution.py:269
  666.5 3.3 copy-start.15
  (41 other events, 46.4 us)
Sparse Core Ops, SparseCore 0:
  10.2 40.4 all-gather.8
  85.5 31.5 all-gather.10
  118.7 45.9 all-gather.12
  166.1 44.6 all-gather.14
  401.5 46.3 reduce-scatter.5
  450.7 23.8 reduce-scatter.9
  477.0 44.6 reduce-scatter.11
  523.9 43.1 reduce-scatter.13
  569.6 34.5 reduce-scatter.7
  608.1 58.3 all-reduce.9
where the time goes:
time: 687 us; the launch traced here: 680 us
  waiting for transfers between devices  240 us (35%)
  blocking collectives  157 us (23%)
  matrix products  124 us (18%)
  local copies, waits for them, and re-layouts  65.7 us (10%)
  other arithmetic  64.5 us (9%)
  between operations  18.4 us (3%)
  starting transfers between devices  9.25 us (1%)
    reduce_scatter x1, waiting for transfers between devices, per_device(): lax.psum_scatter(grad_down.astype(jnp.bfloat16), 'wt', scatter_dimension=...  45.5 us
    psum x1, blocking collectives, per_device(): lax.psum((jnp.sum(valid_float), jnp.sum(valid_float * jnp.sum(distance *...  38.9 us
    reduce_scatter x1, waiting for transfers between devices, per_device(): lax.psum_scatter(grad_pieces.reshape(ctx_count * group_rows, head_count *...  38.5 us
    reduce_scatter x1, waiting for transfers between devices, per_device(): lax.psum_scatter(grad_qkv.astype(jnp.bfloat16), 'wt', scatter_dimension=0...  37.1 us
    psum x1, waiting for transfers between devices, per_device(): lax.psum(shard_qkv.astype(jnp.bfloat16), 'ctx').astype(jnp.float32)  35.2 us
    dot_general x16, matrix products, scores_of(): jnp.einsum('qhd,khd->hqk', queries, kv_piece[:, :, 0], preferred_element_...  32 us
    reduce_scatter x1, waiting for transfers between devices, per_device(): lax.psum_scatter(grad_up.astype(jnp.bfloat16), 'wt', scatter_dimension=0,...  31.3 us
    dot_general x8, matrix products, forward_step(): jnp.einsum('hqk,khd->qhd', weights.astype(jnp.bfloat16), kv_piece[:, :, 1...  30.9 us
  transfers between devices with their start and end apart: 12, of which 8 were waited for; matrix products, arithmetic and copies ran while one was open for 20% of the time, Pallas kernels for 0%

commit v1 on v0

--- a/solution.py
+++ b/solution.py
@@ -149,9 +149,12 @@
     residual_two = residual_one + jnp.dot(activated, down_full, preferred_element_type=jnp.float32)
     distance = residual_two - teacher.astype(jnp.float32)
     valid_float = valid.astype(jnp.float32)
-    count_all, square_all = lax.psum(
-        (jnp.sum(valid_float), jnp.sum(valid_float * jnp.sum(distance * distance, axis=-1))),
-        ("ctx", "wt"),
+    count_all, square_all = jax.lax.psum(
+        jax.lax.psum(
+            (jnp.sum(valid_float), jnp.sum(valid_float * jnp.sum(distance * distance, axis=-1))),
+            "wt",
+        ),
+        "ctx",
     )
     loss_value = square_all / (count_all * model_width)
     grad_two = 2.0 * LOSS_SCALE / (count_all * model_width) * valid_float[:, None] * distance

time: 687 us -> 671 us (0.977)
  blocking collectives: 157 us -> 142 us
    psum x1 -> x2, blocking collectives: 38.9 us -> 24.3 us  [the longest x1 12.4 us: per_device(): jax.lax.psum(jax.lax.psum((jnp.sum(valid_float), jnp.sum(valid_float * jn...]
where the time goes in v1:
time: 671 us; the launch traced here: 664 us
  waiting for transfers between devices  239 us (36%)
  blocking collectives  142 us (21%)
  matrix products  124 us (18%)
  local copies, waits for them, and re-layouts  65.8 us (10%)
  other arithmetic  64.5 us (10%)
  between operations  18.3 us (3%)
  starting transfers between devices  9.12 us (1%)
    reduce_scatter x1, waiting for transfers between devices, per_device(): lax.psum_scatter(grad_down.astype(jnp.bfloat16), 'wt', scatter_dimension=...  45.5 us
    reduce_scatter x1, waiting for transfers between devices, per_device(): lax.psum_scatter(grad_qkv.astype(jnp.bfloat16), 'wt', scatter_dimension=0...  37 us
    reduce_scatter x1, waiting for transfers between devices, per_device(): lax.psum_scatter(grad_pieces.reshape(ctx_count * group_rows, head_count *...  36.5 us
    psum x1, waiting for transfers between devices, per_device(): lax.psum(shard_qkv.astype(jnp.bfloat16), 'ctx').astype(jnp.float32)  35.1 us
    dot_general x16, matrix products, scores_of(): jnp.einsum('qhd,khd->hqk', queries, kv_piece[:, :, 0], preferred_element_...  32 us
    reduce_scatter x1, waiting for transfers between devices, per_device(): lax.psum_scatter(grad_up.astype(jnp.bfloat16), 'wt', scatter_dimension=0,...  31.4 us
    dot_general x8, matrix products, forward_step(): jnp.einsum('hqk,khd->qhd', weights.astype(jnp.bfloat16), kv_piece[:, :, 1...  30.9 us
    all_gather x1, waiting for transfers between devices, per_device(): lax.all_gather(key_values, 'ctx', axis=0, tiled=True)  26.7 us
  transfers between devices with their start and end apart: 12, of which 8 were waited for; matrix products, arithmetic and copies ran while one was open for 20% of the time, Pallas kernels for 0%

profile of v1, /device:TPU:0, one launch (start us, length us, event | category | flops | bytes accessed | tf_op | source)
XLA Modules:
  0.0 663.5 jit_solution(9010410010962687493)
XLA Ops:
  9.3 12.7 %all-gather = bf16[4,1,128]{2,1,0:T(2,128)(2,1)S(1)} all-gather(bf16[1,1,128]{2,1,0:T(2,128)(2,1)} %bitcast.256), channel_id=1, replica_groups=mesh['ctx'=8,'wt'=4] {'wt'}, dimensions={0}, use_global_device_ids=true | all-gather | bytes 1280 | tf_op jit(solution)/shard_map/all_gather | solution.py:52
  22.0 7.8 %all-gather.1 = bf16[4,1,128]{2,1,0:T(2,128)(2,1)S(1)} all-gather(bf16[1,1,128]{2,1,0:T(2,128)(2,1)} %bitcast.257), channel_id=1, replica_groups=mesh['ctx'=8,'wt'=4] {'wt'}, dimensions={0}, use_global_device_ids=true | all-gather | bytes 1280 | tf_op jit(solution)/shard_map/all_gather | solution.py:53
  32.0 18.6 %all-gather.9.cloned.1.call-done = bf16[512,1536]{0,1:T(8,128)(2,1)} async-done(((bf16[128,1536]{0,1:T(8,128)(2,1)}), bf16[512,1536]{0,1:T(8,128)(2,1)}) %all-gather.9.cloned.1.call-update) | async-done | bytes 1572880 | tf_op jit(solution)/shard_map/all_gather | solution.py:50
  53.6 4.4 reduce.16
  58.6 18.8 %all_to_all.40 = bf16[4,2,36864]{2,1,0:T(2,128)(2,1)S(1)} all-to-all(bf16[4,2,36864]{2,1,0:T(2,128)(2,1)S(1)} %reshape.330), channel_id=1, replica_groups=mesh['ctx'=8,'wt'=4] {'wt'}, dimensions={0} | all-to-all | bytes 1179648 | tf_op jit(solution)/shard_map/all_to_all | solution.py:65
  78.0 3.8 reduce.6
  90.4 26.7 %all-gather.11.cloned.1.call-done = bf16[6144,256]{0,1:T(8,128)(2,1)} async-done(((bf16[768,256]{0,1:T(8,128)(2,1)}), bf16[6144,256]{0,1:T(8,128)(2,1)}) %all-gather.11.cloned.1.call-update) | async-done | bytes 3145744 | tf_op jit(solution)/shard_map/all_gather | solution.py:76
  117.1 2.8 copy.143
  122.3 84.7 %while.28 = (s32[]{:T(128)}, f32[2,768]{1,0:T(2,128)S(1)}, f32[2,768]{1,0:T(2,128)S(1)}, f32[768,2,64]{0,2,1:T(8,128)S(1)}, s32[8,768]{1,0:T(8,128)}, /*index=5*...) while((s32[]{:T(128)}, f32[2,768]{1,0:T(2,128)S(1)}, ...), condition=%wide.region_7.8_spmd.clone, body=%wide.region_4.7_spmd.clone.sunk | while | flops 317039616 | bytes 37675172 | solution.py:121
  124.6 3.2 fusion.119
  127.8 3.8 fusion.123
  135.2 3.2 fusion.119
  138.4 3.8 fusion.123
  145.7 3.2 fusion.119
  148.9 3.8 fusion.123
  156.3 3.2 fusion.119
  159.5 3.8 fusion.123
  166.8 3.2 fusion.119
  170.0 4.1 fusion.123
  177.8 3.2 fusion.119
  181.0 3.8 fusion.123
  188.3 3.2 fusion.119
  191.5 3.9 fusion.123
  198.9 3.2 fusion.119
  202.1 3.8 fusion.123
  213.4 4.5 all-to-all-start.1
  217.9 11.3 %all-gather.2 = bf16[4,1,128]{2,1,0:T(2,128)(2,1)S(1)} all-gather(bf16[1,1,128]{2,1,0:T(2,128)(2,1)S(1)} %bitcast.258), channel_id=1, replica_groups=mesh['ctx'=8,'wt'=4] {'wt'}, dimensions={0}, use_global_device_ids=true | all-gather | bytes 1280 | tf_op jit(solution)/shard_map/all_gather | solution.py:140
  229.2 7.7 %all-gather.3 = bf16[4,1,128]{2,1,0:T(2,128)(2,1)S(1)} all-gather(bf16[1,1,128]{2,1,0:T(2,128)(2,1)S(1)} %bitcast.259), channel_id=1, replica_groups=mesh['ctx'=8,'wt'=4] {'wt'}, dimensions={0}, use_global_device_ids=true | all-gather | bytes 1280 | tf_op jit(solution)/shard_map/all_gather | solution.py:141
  236.9 15.0 %all_gather.31 = bf16[512,512]{1,0:T(8,128)(2,1)S(1)} all-gather(bf16[128,512]{1,0:T(8,128)(2,1)S(1)} %copy-done.20), channel_id=1, replica_groups=mesh['ctx'=8,'wt'=4] {'wt'}, dimensions={0}, use_global_device_ids=true | all-gather | bytes 655360 | tf_op jit(solution)/shard_map/all_gather | solution.py:51
  254.0 6.9 %multiply_convert_fusion = (bf16[192,2048]{1,0:T(8,128)(2,1)}, f32[192,2048]{1,0:T(8,128)}, f32[192,2048]{1,0:T(8,128)}) fusion(bf16[512,2048]{1,0:T(8,128)(2,1)} %all-gather.13.cloned.1.call-done, f32[192,512]{1,0:T(8,128)S(1)} %get-tuple-element.402, f32[512]{0:T(512)S(1)} %bitcast.253, f32[512]{0:T(512)S(1)} %bitcast.249, f32[192]{0:T(256)S(1)} %add_rsqrt_fusion, ...), kind=kOutput, calls=%fused_computation.55 | convolution fusion | flops 428703744 | bytes 6428160 | tf_op jit(solution)/shard_map/dot_general | solution.py:147
  264.1 11.8 %all-reduce.5 = (f32[]{:T(128)}, f32[]{:T(128)}) all-reduce(f32[]{:T(128)} %get-tuple-element.324, f32[]{:T(128)} %get-tuple-element.323), channel_id=1, replica_groups=mesh['ctx'=8,'wt'=4] {'wt'}, use_global_device_ids=true, to_apply=%region_12.13 | all-reduce | flops 2 | bytes 16 | tf_op jit(solution)/shard_map/psum | solution.py:153
  275.9 12.4 %all-reduce.4 = (f32[]{:T(128)}, f32[]{:T(128)}) all-reduce(f32[]{:T(128)} %get-tuple-element.371, f32[]{:T(128)} %get-tuple-element.372), channel_id=1, replica_groups=mesh['ctx'=8,'wt'=4] {'ctx'}, use_global_device_ids=true, to_apply=%region_13.14 | all-reduce | flops 2 | bytes 16 | tf_op jit(solution)/shard_map/psum | solution.py:152
  289.2 3.7 add_convert_fusion
  298.6 3.4 all-to-all-start.2
  303.1 6.6 all-to-all-done.2
  314.1 66.9 %while.29 = (s32[]{:T(128)}, f32[768,2,64]{0,2,1:T(8,128)S(1)}, bf16[8,768,2,2,64]{1,4,2,3,0:T(8,128)(2,1)}, bf16[8,768,2,2,64]{1,4,2,3,0:T(8,128)(2,1)}, s32[8,...) while((s32[]{:T(128)}, f32[768,2,64]{0,2,1:T(8,128)S(1)}, ...), condition=%wide.region_21.22_spmd.clone, body=%wide.region_20.21_spmd.clone.sunk | while | flops 769720320 | bytes 28011244 | solution.py:214
  381.0 3.6 copy.129
  384.7 2.6 copy.145
  395.2 36.5 %reduce-scatter.6.cloned.1.call-done = bf16[768,256]{0,1:T(8,128)(2,1)} async-done(((bf16[6144,256]{0,1:T(8,128)(2,1)}), bf16[768,256]{0,1:T(8,128)(2,1)}) %reduce-scatter.6.cloned.1.call-update) | async-done | bytes 393232 | tf_op jit(solution)/shard_map/reduce_scatter | solution.py:217
  436.0 5.6 reduce.19
  442.2 23.0 %all_to_all.41 = bf16[4,2,36864]{2,1,0:T(2,128)(2,1)S(1)} all-to-all(bf16[4,2,36864]{2,1,0:T(2,128)(2,1)S(1)} %reshape.336), channel_id=1, replica_groups=mesh['ctx'=8,'wt'=4] {'wt'}, dimensions={0} | all-to-all | bytes 1179648 | tf_op jit(solution)/shard_map/all_to_all | solution.py:226
  465.8 3.8 reduce.9
  474.1 31.4 %reduce-scatter.12.cloned.1.call-done = bf16[128,2048]{1,0:T(8,128)(2,1)} async-done(((bf16[512,2048]{1,0:T(8,128)(2,1)}), bf16[128,2048]{1,0:T(8,128)(2,1)}) %reduce-scatter.12.cloned.1.call-update) | async-done | bytes 524304 | tf_op jit(solution)/shard_map/reduce_scatter | solution.py:262
  505.5 45.5 %reduce-scatter.14.cloned.1.call-done = bf16[512,512]{1,0:T(8,128)(2,1)} async-done(((bf16[2048,512]{1,0:T(8,128)(2,1)}), bf16[512,512]{1,0:T(8,128)(2,1)}) %reduce-scatter.14.cloned.1.call-update) | async-done | bytes 524304 | tf_op jit(solution)/shard_map/reduce_scatter | solution.py:265
  551.0 37.0 %reduce-scatter.8.cloned.1.call-done = bf16[128,1536]{1,0:T(8,128)(2,1)} async-done(((bf16[512,1536]{1,0:T(8,128)(2,1)}), bf16[128,1536]{1,0:T(8,128)(2,1)}) %reduce-scatter.8.cloned.1.call-update) | async-done | bytes 393232 | tf_op jit(solution)/shard_map/reduce_scatter | solution.py:250
  590.2 9.8 %all-reduce.8 = (bf16[512]{0:T(512)(128)(2,1)S(1)}, bf16[512]{0:T(512)(128)(2,1)S(1)}, bf16[512]{0:T(512)(128)(2,1)S(1)}, bf16[512]{0:T(512)(128)(2,1)S(1)}) all-reduce(bf16[512]{0:T(512)(128)(2,1)S(1)} %get-tuple-element.317, bf16[512]{0:T(512)(128)(2,1)S(1)} %get-tuple-element.322, ...), channel_id=3, replica_groups=mesh['ctx'=8,'wt'=4] {'wt'}, use_global_device_ids=true, to_apply=%region_26.27.clone | all-reduce | flops 2048 | bytes 8192
  600.3 11.9 %all-reduce.6 = (bf16[128]{0:T(256)(128)(2,1)S(1)}, bf16[128]{0:T(256)(128)(2,1)S(1)}, bf16[128]{0:T(256)(128)(2,1)S(1)}, bf16[128]{0:T(256)(128)(2,1)S(1)}) all-reduce(bf16[128]{0:T(256)(128)(2,1)S(1)} %dynamic-slice.1, bf16[128]{0:T(256)(128)(2,1)S(1)} %dynamic-slice.3, ...), channel_id=1, replica_groups=mesh['ctx'=8,'wt'=4] {'ctx'}, use_global_device_ids=true, to_apply=%region_27.28 | all-reduce | flops 512 | bytes 2048 | tf_op jit(solution)/shard_map/psum | solution.py:270
  615.2 35.1 %all-reduce.11.cloned.1.call-done = (bf16[128,1536]{1,0:T(8,128)(2,1)}, bf16[128,512]{1,0:T(8,128)(2,1)}, bf16[128,2048]{1,0:T(8,128)(2,1)}, bf16[512,512]{1,0:T(8,128)(2,1)}) async-done(((bf16[128,1536]{1,0:T(8,128)(2,1)}, bf16[128,512]{1,0:T(8,128)(2,1)}, bf16[128,2048]{1,0:T(8,128)(2,1)}, bf16[512,512]{1,0:T(8,128)(2,1)}), (bf16[128,1536]{1,0:T(8,128)(2,1)}, bf16[128,512]{1,0:T(8,128)(2,1)}, ...) | async-done | bytes 1572880 | tf_op jit(solution)/shard_map/psum | solution.py:272
  (403 shorter events, 163.0 us)
Async XLA Ops:
  7.2 43.5 %copy-start.3 = (bf16[192,512]{1,0:T(8,128)(2,1)S(1)}, bf16[192,512]{1,0:T(8,128)(2,1)}, u32[]{:S(2)}) copy-start(bf16[192,512]{1,0:T(8,128)(2,1)} %param.17) | copy-start | bytes 589828
  7.2 43.4 %all-gather.9.cloned.1.call-start = ((), (), s32[]{:S(2)}) async-start(), calls=%async_computation.9 | async-start | bytes 1966080 | tf_op jit(solution)/shard_map/all_gather | solution.py:50
  9.2 107.9 %all-gather.11.cloned.1.call-start = ((), (), s32[]{:S(2)}) async-start(), calls=%async_computation.10 | async-start | bytes 3538944 | tf_op jit(solution)/shard_map/all_gather | solution.py:76
  22.0 28.6 %copy-start.22 = (f32[4,1,128]{2,1,0:T(1,128)}, f32[4,1,128]{2,1,0:T(1,128)S(1)}, u32[]{:S(2)}) copy-start(f32[4,1,128]{2,1,0:T(1,128)S(1)} %convert_element_type.187) | copy-start | bytes 6148
  29.8 20.8 %copy-start.26 = (f32[4,1,128]{2,1,0:T(1,128)}, f32[4,1,128]{2,1,0:T(1,128)S(1)}, u32[]{:S(2)}) copy-start(f32[4,1,128]{2,1,0:T(1,128)S(1)} %convert_element_type.188) | copy-start | bytes 6148
  30.8 19.8 %copy-start.24 = (f32[192]{0:T(256)}, f32[192]{0:T(256)S(1)}, u32[]{:S(2)}) copy-start(f32[192]{0:T(256)S(1)} %broadcast_multiply_fusion.5) | copy-start | bytes 2308
  32.0 18.6 %copy-start.32 = (f32[192]{0:T(256)}, f32[192]{0:T(256)S(1)}, u32[]{:S(2)}) copy-start(f32[192]{0:T(256)S(1)} %add_rsqrt_fusion.1) | copy-start | bytes 2308
  83.7 3.1 copy-start.46
  83.7 3.5 copy-start.47
  85.4 168.6 %all-gather.13.cloned.1.call-start = ((), (), s32[]{:S(2)}) async-start(), calls=%async_computation.11 | async-start | bytes 2621440 | tf_op jit(solution)/shard_map/all_gather | solution.py:138
  86.1 174.8 %all-gather.15.cloned.1.call-start = ((), (), s32[]{:S(2)}) async-start(), calls=%async_computation.12 | async-start | bytes 2621440 | tf_op jit(solution)/shard_map/all_gather | solution.py:139
  127.8 3.8 copy-start
  138.4 3.8 copy-start
  148.9 3.8 copy-start
  159.5 3.8 copy-start
  170.0 4.3 copy-start
  181.0 3.8 copy-start
  191.5 3.9 copy-start
  202.1 3.8 copy-start
  207.1 3.3 copy-start.17
  210.4 7.5 %copy-start.43 = (bf16[128]{0:T(256)(128)(2,1)S(1)}, bf16[128]{0:T(256)(128)(2,1)}, u32[]{:S(2)}) copy-start(bf16[128]{0:T(256)(128)(2,1)} %param.26) | copy-start | bytes 772
  210.4 18.9 %copy-start.44 = (bf16[128]{0:T(256)(128)(2,1)S(1)}, bf16[128]{0:T(256)(128)(2,1)}, u32[]{:S(2)}) copy-start(bf16[128]{0:T(256)(128)(2,1)} %param.27) | copy-start | bytes 772
  210.4 26.5 %copy-start.20 = (bf16[128,512]{1,0:T(8,128)(2,1)S(1)}, bf16[128,512]{1,0:T(8,128)(2,1)}, u32[]{:S(2)}) copy-start(bf16[128,512]{1,0:T(8,128)(2,1)} %param.25) | copy-start | bytes 393220
  213.4 38.5 %all-to-all-start.1 = ((bf16[4,2,12288]{2,1,0:T(2,128)(2,1)}), bf16[4,2,12288]{2,1,0:T(2,128)(2,1)S(1)}, u32[]{:S(2)}, u32[]{:S(2)}) async-start(bf16[4,2,12288]{2,1,0:T(2,128)(2,1)} %reshape.332), calls=%async_computation.1 | async-start | bytes 393216 | tf_op jit(solution)/shard_map/all_to_all | solution.py:127
  229.2 65.2 %copy-start.28 = (f32[4,1,128]{2,1,0:T(1,128)}, f32[4,1,128]{2,1,0:T(1,128)S(1)}, u32[]{:S(2)}) copy-start(f32[4,1,128]{2,1,0:T(1,128)S(1)} %convert_element_type.189) | copy-start | bytes 6148
  236.9 17.1 %copy-start.36 = (f32[4,1,128]{2,1,0:T(1,128)}, f32[4,1,128]{2,1,0:T(1,128)S(1)}, u32[]{:S(2)}) copy-start(f32[4,1,128]{2,1,0:T(1,128)S(1)} %convert_element_type.190) | copy-start | bytes 6148
  253.4 7.6 %copy-start.8 = (bf16[4,24576]{1,0:T(4,128)(2,1)}, bf16[4,24576]{1,0:T(4,128)(2,1)S(1)}, u32[]{:S(2)}) copy-start(bf16[4,24576]{1,0:T(4,128)(2,1)S(1)} %reduce.7) | copy-start | bytes 589828
  253.7 40.7 %copy-start.1 = (f32[192,512]{1,0:T(8,128)}, f32[192,512]{1,0:T(8,128)S(1)}, u32[]{:S(2)}) copy-start(f32[192,512]{1,0:T(8,128)S(1)} %get-tuple-element.402) | copy-start | bytes 1179652
  253.8 40.7 %copy-start.30 = (f32[192]{0:T(256)}, f32[192]{0:T(256)S(1)}, u32[]{:S(2)}) copy-start(f32[192]{0:T(256)S(1)} %broadcast_multiply_fusion.4) | copy-start | bytes 2308
  254.0 40.5 %copy-start.34 = (f32[192]{0:T(256)}, f32[192]{0:T(256)S(1)}, u32[]{:S(2)}) copy-start(f32[192]{0:T(256)S(1)} %add_rsqrt_fusion) | copy-start | bytes 2308
  254.0 6.9 %copy-start.7 = (bf16[192,512]{1,0:T(8,128)(2,1)S(1)}, bf16[192,512]{1,0:T(8,128)(2,1)}, u32[]{:S(2)}) copy-start(bf16[192,512]{1,0:T(8,128)(2,1)} %param.18) | copy-start | bytes 589828
  261.0 2.6 copy-start.40
  289.2 3.7 copy-start.10
  289.2 3.7 copy-start.45
  295.4 14.5 %copy-start.4 = (f32[192,512]{1,0:T(8,128)}, f32[192,512]{1,0:T(8,128)S(1)}, u32[]{:S(2)}) copy-start(f32[192,512]{1,0:T(8,128)S(1)} %get-tuple-element.397) | copy-start | bytes 1179652
  295.4 7.1 %copy-start.18 = (f32[2,768]{1,0:T(2,128)S(1)}, f32[2,768]{1,0:T(2,128)}, u32[]{:S(2)}) copy-start(f32[2,768]{1,0:T(2,128)} %copy-done.17) | copy-start | bytes 18436
  298.6 11.1 %all-to-all-start.2 = ((bf16[4,2,12288]{2,1,0:T(2,128)(2,1)}), bf16[4,2,12288]{2,1,0:T(2,128)(2,1)S(1)}, u32[]{:S(2)}, u32[]{:S(2)}) async-start(bf16[4,2,12288]{2,1,0:T(2,128)(2,1)} %reshape.334), calls=%async_computation.2 | async-start | bytes 393216 | tf_op jit(solution)/shard_map/all_to_all | solution.py:179
  302.0 129.7 %reduce-scatter.6.cloned.1.call-start = ((), (), s32[]{:S(2)}) async-start(), calls=%async_computation.13 | async-start | bytes 3538944 | tf_op jit(solution)/shard_map/reduce_scatter | solution.py:217
  387.3 2.2 copy-start.2
  387.3 2.2 copy-start.13
  387.3 2.2 copy-start.29
  387.3 2.2 copy-start.31
  387.3 86.8 %reduce-scatter.10.cloned.1.call-start = ((), (), s32[]{:S(2)}) async-start(), calls=%async_computation.15 | async-start | bytes 655360 | tf_op jit(solution)/shard_map/reduce_scatter | solution.py:253
  389.4 116.1 %reduce-scatter.12.cloned.1.call-start = ((), (), s32[]{:S(2)}) async-start(), calls=%async_computation.16 | async-start | bytes 2621440 | tf_op jit(solution)/shard_map/reduce_scatter | solution.py:262
  391.8 159.3 %reduce-scatter.14.cloned.1.call-start = ((), (), s32[]{:S(2)}) async-start(), calls=%async_computation.17 | async-start | bytes 2621440 | tf_op jit(solution)/shard_map/reduce_scatter | solution.py:265
  395.1 192.9 %reduce-scatter.8.cloned.1.call-start = ((), (), s32[]{:S(2)}) async-start(), calls=%async_computation.14 | async-start | bytes 1966080 | tf_op jit(solution)/shard_map/reduce_scatter | solution.py:250
  472.2 178.2 %all-reduce.11.cloned.1.call-start = ((), (), s32[]{:S(2)}) async-start(), calls=%async_computation.18 | async-start | bytes 3145728 | tf_op jit(solution)/shard_map/psum | solution.py:272
  650.4 3.3 copy-start.15
  (41 other events, 46.4 us)
Sparse Core Ops, SparseCore 0:
  10.2 40.4 all-gather.8
  85.5 31.5 all-gather.10
  118.7 45.9 all-gather.12
  166.1 44.6 all-gather.14
  387.4 44.2 reduce-scatter.5
  434.5 23.9 reduce-scatter.9
  460.8 44.6 reduce-scatter.11
  507.8 43.1 reduce-scatter.13
  553.5 34.5 reduce-scatter.7
  591.9 58.4 all-reduce.10
